TPU v7x, 32 devices: a whole 2x2x4 slice. The times are simulated.
32 devices in a mesh: ex: 4 (over z), ey: 2 (over y), ez: 4 (over x, core).
Axes of the slice: x: 2, y: 2, z: 4, core: 2. Of those that a mesh axis runs over, the one named last changes fastest.
Arguments:
- residual: float32 [64, 32, 512], P('ez', 'ey', 'ex'), may hold values from -6 to 6
- local_stream: float32 [18, 18], replicated, may hold values from -1.5 to 1.5
- local_normal: float32 [2, 18, 18], P('ey'), may hold values from -1.5 to 1.5
- local_span: float32 [18, 18], replicated, may hold values from -1.5 to 1.5
- eigen_stream: float32 [18], replicated, may hold values from 0.3 to 3
- eigen_normal: float32 [2, 18], P('ey'), may hold values from 0.3 to 3
- eigen_span: float32 [18], replicated, may hold values from 0.3 to 3
- vertex_stream: float32 [32, 32], replicated, may hold values from -1 to 1
- vertex_normal: float32 [2, 2], replicated, may hold values from -4 to 4
- vertex_span: float32 [4, 4], replicated, may hold values from -3 to 3
- level_stream: float32 [32], replicated, may hold values from 4 to 40
- level_normal: float32 [2], replicated, may hold values from 4 to 40
- level_span: float32 [4], replicated, may hold values from 4 to 40
Outputs:
- applied: float32 [64, 32, 512], P('ez', 'ey', 'ex')
All inputs are finite; a program needn't handle non-finite values.
Results may differ from a plain program's by a relative error of at most 0.0003.
Values sent between devices are 32-bit elements; how exact they have to be, the bound alone decides.
A program may use at most 64 MiB of HBM per device.

v0:
```python
import functools
import math

import jax
import jax.numpy as jnp
from jax import lax
from jax.experimental import pallas as pl
from jax.experimental.pallas import tpu as pltpu
from jax.sharding import PartitionSpec as P

F32 = jnp.float32
BF16 = jnp.bfloat16
I32 = jnp.int32
HALO = 24
DIRS = ((1, 0), (-1, 0), (0, 1), (0, -1), (1, 1), (1, -1), (-1, 1), (-1, -1))


def iota(shape, dim):
    return lax.broadcasted_iota(I32, shape, dim)


def quotient(x, d):
    return (x * (65536 // d + 1)) >> 16


def onehot(mask):
    return jnp.where(mask, 1.0, 0.0).astype(F32)


def split(x):
    hi = x.astype(BF16)
    return hi, (x - hi.astype(F32)).astype(BF16)


def dg(a, b, dims):
    return lax.dot_general(a, b, ((dims[:1], dims[1:]), ((), ())), preferred_element_type=F32)


def dot3(a, b, dims=(1, 0)):
    (ah, al), (bh, bl) = a, b
    return dg(ah, bh, dims) + (dg(ah, bl, dims) + dg(al, bh, dims))


def pick(mask, values, dims=(1, 0)):
    hi, lo = split(values)
    mask = mask.astype(BF16)
    return dg(mask, hi, dims) + dg(mask, lo, dims)


def hat(index, points):
    out = jnp.zeros(index.shape, F32)
    for i in range(points):
        out = jnp.where(index == i, (1.0 - math.cos(math.pi * i / (points - 1))) / 2.0, out)
    return out


def kernel(
    sizes,
    res, stream, normal, span, eig_x, eig_y, eig_z,
    v_stream, v_normal, v_span, lev_x, lev_y, lev_z,
    out,
    rim, kh, kl, cx, back, got, parts, mine,
    ssem, rsem,
):
    nx, ny, nz = sizes
    block = stream.shape[0]
    n = block - 2
    sh = n.bit_length() - 1
    length = res.shape[2]
    ne = length // n
    main = n * n
    rows = kh.shape[0]
    nrim = rows - main
    lanes = kh.shape[1]
    edge = main + 4 * n
    nv, nm = v_stream.shape
    mn = nz * ny
    ix, iy, iz = lax.axis_index("ex"), lax.axis_index("ey"), lax.axis_index("ez")

    rim[...] = jnp.zeros_like(rim)
    got[...] = jnp.zeros_like(got)

    def wrap(i, size):
        return lax.rem(i + size, size)

    def has(dy):
        return jnp.logical_and(iy + dy >= 0, iy + dy < ny)

    def guarded(dy, fn):
        if dy == 0:
            fn()
        else:
            pl.when(has(dy))(fn)

    barrier = pltpu.get_barrier_semaphore()

    def signal(where):
        pl.semaphore_signal(
            barrier, inc=1, device_id=where, device_id_type=pl.DeviceIdType.MESH
        )

    for axis, index, size in (("ez", iz, nz), ("ey", iy, ny), ("ex", ix, nx)):
        for d in range(1, size):
            signal({axis: lax.rem(index + d, size)})
    for dz, dy in DIRS[4:]:
        guarded(dy, functools.partial(signal, {"ez": wrap(iz + dz, nz), "ey": iy + dy}))
    inner = jnp.where(iy > 0, 2, 0) + jnp.where(iy < ny - 1, 2, 0)

    data = res[...].reshape(main, length)
    row, col = iota((rows, block), 0), iota((rows, block), 1)
    low = row & (n - 1)
    e0 = row - edge
    rk = jnp.where(row < main, (row >> sh) + 1, low + 1)
    rk = jnp.where((row >= main) & (row < main + n), 0, rk)
    rk = jnp.where((row >= main + n) & (row < main + 2 * n), n + 1, rk)
    rk = jnp.where(row >= edge, jnp.where(e0 < 2, 0, n + 1), rk)
    rk = jnp.where(row >= edge + 4, -1, rk)
    rj = jnp.where((row >= main + 2 * n) & (row < main + 3 * n), 0, low + 1)
    rj = jnp.where((row >= main + 3 * n) & (row < main + 4 * n), n + 1, rj)
    rj = jnp.where(row >= edge, jnp.where((e0 & 1) == 0, 0, n + 1), rj)
    rj = jnp.where(row >= edge + 4, -1, rj)
    sel_k, sel_j = onehot(rk == col), onehot(rj == col)
    brow, bcol = iota((block, lanes), 0), iota((block, lanes), 1)
    bq = quotient(bcol, block)
    to_r = onehot(bq == brow)
    to_q = onehot((bcol - block * bq == brow) & (bcol < block * block))
    span_l = dot3(split(span[...]), split(to_r))
    normal_l = dot3(split(normal[0]), split(to_q))
    kmat = pick(sel_k, span_l) * pick(sel_j, normal_l)
    k_hi, k_lo = split(kmat)
    kh[...] = k_hi
    kl[...] = k_lo

    wn = n
    hrow, hcol = iota((8, main), 0), iota((8, main), 1)
    wk, wj = hat(hcol >> sh, wn), hat(hcol & (n - 1), wn)
    hyz = jnp.where((hrow & 2) > 0, wk, 1.0 - wk) * jnp.where((hrow & 1) > 0, wj, 1.0 - wj)
    hyz = split(jnp.where(hrow < 4, hyz, 0.0))
    xrow, xcol = iota((length, nv), 0), iota((length, nv), 1)
    wx = hat(xrow & (n - 1), wn)
    base = ix * ne + (xrow >> sh)
    after = jnp.where(base + 1 >= nv, base + 1 - nv, base + 1)
    hx = jnp.where(xcol == base, 1.0 - wx, 0.0) + jnp.where(xcol == after, wx, 0.0)
    wxm = split(dot3(split(hx), split(v_stream[...])))
    d_split = split(data)
    loads = dot3(split(dot3(hyz, d_split)), wxm)
    mrow, mcol = iota((mn, nz), 0), iota((mn, nz), 1)
    is_m = onehot((mrow >= mcol * ny) & (mrow < (mcol + 1) * ny))
    nrow, ncol = iota((mn, ny), 0), iota((mn, ny), 1)
    is_n = onehot(nrow - ny * quotient(nrow, ny) == ncol)
    vrow, vcol = iota((nz, 8), 0), iota((nz, 8), 1)
    vz = iz + (vcol >> 1)
    vz = jnp.where(vz >= nz, vz - nz, vz)
    at_z = onehot((vrow == vz) & (vcol < 4))
    urow, ucol = iota((ny, 8), 0), iota((ny, 8), 1)
    at_y = onehot((urow == iy + (ucol & 1)) & (ucol < 4))
    amat = pick(is_m, dot3(split(v_span[...].T), split(at_z)))
    amat = amat * pick(is_n, dot3(split(v_normal[...].T), split(at_y)))
    a_split = split(amat)
    mine[0, :, :nm] = dot3(a_split, split(loads))
    level = jnp.sum(is_m * lev_z[...], axis=1, keepdims=True)
    level = level + jnp.sum(is_n * lev_y[...], axis=1, keepdims=True) + lev_x[...]

    pl.semaphore_wait(barrier, (nx - 1) + (ny - 1) + (nz - 1) + inner)

    def shipped(src, dst, slot, where):
        return pltpu.make_async_remote_copy(
            src_ref=src, dst_ref=dst, send_sem=ssem.at[slot], recv_sem=rsem.at[slot],
            device_id=where, device_id_type=pl.DeviceIdType.MESH,
        )

    def target(dz, dy):
        where = {}
        if dz:
            where["ez"] = wrap(iz + dz, nz)
        if dy:
            where["ey"] = iy + dy
        return where

    def halo(slot):
        dz, dy = DIRS[slot]
        if dy == 0:
            src = res.at[n - 1 if dz > 0 else 0]
            dst = rim.at[pl.ds(0 if dz > 0 else n, n)]
        elif dz == 0:
            src = res.at[:, n - 1 if dy > 0 else 0]
            dst = rim.at[pl.ds(2 * n if dy > 0 else 3 * n, n)]
        else:
            src = res.at[n - 1 if dz > 0 else 0, pl.ds(n - 1 if dy > 0 else 0, 1)]
            dst = rim.at[pl.ds(4 * n + (0 if dz > 0 else 2) + (0 if dy > 0 else 1), 1)]
        return shipped(src, dst, slot, target(dz, dy))

    def ret(slot):
        dz, dy = DIRS[slot]
        if dy == 0:
            at, number = (n if dz > 0 else 0), n
        elif dz == 0:
            at, number = (3 * n if dy > 0 else 2 * n), n
        else:
            at, number = 4 * n + (2 if dz > 0 else 0) + (1 if dy > 0 else 0), 1
        return shipped(
            back.at[pl.ds(at, number)], got.at[pl.ds(at, number)], 8 + slot, target(dz, dy)
        )

    def start_all(make):
        for s, (dz, dy) in enumerate(DIRS):
            guarded(dy, lambda s=s: make(s).start())

    def wait_all(make):
        for s, (dz, dy) in enumerate(DIRS):
            guarded(dy, lambda s=s: make(s).wait_send())
            guarded(-dy, lambda s=s: make(s).wait_recv())

    stages = {"ez": (0, iz, nz), "ex": (1, ix, nx), "ey": (2, iy, ny)}
    offset = {"ez": 0, "ex": nz - 1, "ey": nz + nx - 2}

    def stage_copies(axis):
        st, index, size = stages[axis]
        return [
            shipped(
                mine.at[st], parts.at[offset[axis] + d - 1], 18 + offset[axis] + d - 1,
                {axis: lax.rem(index + d, size)},
            )
            for d in range(1, size)
        ]

    def stage_start(axis):
        for c in stage_copies(axis):
            c.start()

    def stage_end(axis):
        st, index, size = stages[axis]
        total = mine[st, :, :nm]
        for d, c in enumerate(stage_copies(axis)):
            c.wait_recv()
            c.wait_send()
            total = total + parts[offset[axis] + d, :, :nm]
        return total

    start_all(halo)
    stage_start("ez")
    k_main = kh[0:main], kl[0:main]
    k_rim = kh[main:], kl[main:]
    c_main = dot3(split(data.T), k_main)
    nep = cx.shape[0]
    pairs = (ne + 2) * block
    npad = -(-pairs // 16) * 16
    wrow, wcol = iota((npad, nep), 0), iota((npad, nep), 1)
    xs = jnp.where(wcol < length, wcol, jnp.where(wcol < length + HALO, wcol - length - HALO, wcol - HALO))
    xi = xs + 1 + n - n * quotient(wrow, block)
    trow, tcol = iota((block, nep), 0), iota((block, nep), 1)
    tx = jnp.where(tcol < length, tcol, jnp.where(tcol < length + HALO, tcol - length - HALO, tcol - HALO))
    tm = (tx + 1) & (n - 1)
    s_t = split(stream[...].T)
    first = dot3(s_t, split(onehot(trow == tm)))
    second = dot3(s_t, split(onehot(trow - n == tm)))
    prow, pcol = iota((npad, block), 0), iota((npad, block), 1)
    is_p = onehot((prow - block * quotient(prow, block) == pcol) & (prow < pairs))
    wmat = jnp.where((xi >= 0) & (xi < n), pick(is_p, first), 0.0)
    wmat = wmat + jnp.where((xi >= n) & (xi < block), pick(is_p, second), 0.0)
    w_main = split(wmat[:, :length])
    w_halo = split(wmat[:, length:])
    w_back = split(wmat[:, :length].T)
    eig_yz = dot3(split(jnp.broadcast_to(eig_z[...], (8, block))), split(to_r))
    eig_yz = eig_yz + dot3(split(jnp.broadcast_to(eig_y[...], (8, block))), split(to_q))
    ecol = jnp.sum(is_p * eig_x[...], axis=1, keepdims=True)
    ecol = jnp.where(iota((npad, 1), 0) < pairs, ecol, 1.0)
    inverse = 1.0 / (ecol + eig_yz[0:1])

    wait_all(halo)
    cx[0:length] = c_main + dot3(split(rim[...].T), k_rim)

    def x_copies():
        right = {"ex": wrap(ix + 1, nx)}
        left = {"ex": wrap(ix - 1, nx)}
        return (
            shipped(cx.at[pl.ds(length - HALO, HALO)], cx.at[pl.ds(length, HALO)], 16, right),
            shipped(cx.at[pl.ds(0, HALO)], cx.at[pl.ds(length + HALO, HALO)], 17, left),
        )

    for c in x_copies():
        c.start()
    mine[1, :, :nm] = stage_end("ez")
    stage_start("ex")
    modal = dot3(w_main, split(cx[0:length]))
    for c in x_copies():
        c.wait()
    modal = modal + dot3(w_halo, split(cx[length:]))
    u = split(dot3(w_back, split(modal * inverse)))
    back[...] = dot3(k_rim, u, (1, 1))
    start_all(ret)
    mine[2, :, :nm] = stage_end("ex")
    stage_start("ey")
    result = dot3(k_main, u, (1, 1))
    scaled = split(stage_end("ey") / level)
    coarse = dot3(split(amat.T), scaled)
    coarse = dot3(split(coarse), wxm, (1, 1))
    result = result + dot3(hyz, split(coarse), (0, 0))
    out[...] = result.reshape(n, n, length)
    wait_all(ret)
    out[n - 1] += got[0:n]
    out[0] += got[n : 2 * n]
    out[:, n - 1] += got[2 * n : 3 * n]
    out[:, 0] += got[3 * n : 4 * n]
    for e in range(4):
        k, j = (n - 1, 0)[e >> 1], (n - 1, 0)[e & 1]
        out[k, j : j + 1] += got[4 * n + e : 4 * n + e + 1]


def per_device(sizes, residual, local_stream, local_normal, local_span, eigen_stream, eigen_normal,
               eigen_span, vertex_stream, vertex_normal, vertex_span, level_stream, level_normal,
               level_span):
    nx, ny, nz = sizes
    block = local_stream.shape[0]
    n = block - 2
    length = residual.shape[2]
    rows = n * n + 4 * n + 16
    lanes = -(-block * block // 128) * 128
    mn = ny * nz
    copies = 18 + nx + ny + nz - 3
    vmem = pl.BlockSpec(memory_space=pltpu.VMEM)
    return pl.pallas_call(
        functools.partial(kernel, sizes),
        out_shape=jax.ShapeDtypeStruct(residual.shape, F32),
        in_specs=[vmem] * 13,
        out_specs=vmem,
        scratch_shapes=[
            pltpu.VMEM((rows - n * n, length), F32),
            pltpu.VMEM((rows, lanes), BF16),
            pltpu.VMEM((rows, lanes), BF16),
            pltpu.VMEM((length + 2 * HALO, lanes), F32),
            pltpu.VMEM((rows - n * n, length), F32),
            pltpu.VMEM((rows - n * n, length), F32),
            pltpu.VMEM((nx + ny + nz - 3, mn, 128), F32),
            pltpu.VMEM((3, mn, 128), F32),
            pltpu.SemaphoreType.DMA((copies,)),
            pltpu.SemaphoreType.DMA((copies,)),
        ],
        compiler_params=pltpu.CompilerParams(collective_id=0, has_side_effects=True),
    )(
        residual, local_stream, local_normal, local_span, eigen_stream.reshape(1, -1), eigen_normal,
        eigen_span.reshape(1, -1), vertex_stream, vertex_normal, vertex_span,
        level_stream.reshape(1, -1), level_normal.reshape(1, -1), level_span.reshape(1, -1),
    )


def solution(mesh):
    sizes = (mesh.shape["ex"], mesh.shape["ey"], mesh.shape["ez"])
    placed = (P("ez", "ey", "ex"), P(), P("ey", None, None), P(), P(), P("ey", None)) + (P(),) * 7
    return jax.shard_map(
        functools.partial(per_device, sizes), mesh=mesh, in_specs=placed,
        out_specs=P("ez", "ey", "ex"), check_vma=False,
    )
```

profile of v0, /device:TPU:0, one launch (start us, length us, event | category | flops | bytes accessed | tf_op | source)
XLA Modules:
  0.0 21.9 jit_solution(14486924310452289217)
XLA Ops:
  0.0 0.0 copy-start
  0.0 0.7 %copy-done = f32[1,18,18]{2,0,1:T(1,128)S(1)} copy-done((f32[1,18,18]{2,0,1:T(1,128)S(1)}, f32[1,18,18]{2,0,1:T(1,128)}, u32[]{:S(2)}) %copy-start) | copy-done | bytes 1320
  0.7 0.6 %copy.14.normal = f32[1,18,18]{2,1,0:T(8,128)} copy(f32[1,18,18]{2,0,1:T(1,128)S(1)} %copy-done) | data formatting | bytes 2592 | tf_op args[2]
  1.3 19.0 %shard_map.127 = f32[16,16,128]{2,1,0:T(8,128)} custom-call(f32[16,16,128]{2,1,0:T(8,128)} %res.1, f32[18,18]{1,0:T(8,128)} %stream.1, f32[1,18,18]{2,1,0:T(8,128)} %copy.14.normal, f32[18,18]{1,0:T(8,128)} %span.1, f32[1,18]{1,0:T(1,128)} %bitcast.5, f32[1,18]{1,0:T(1,128)} %eig_y.1, f32[1,18]{1,0:T(1,128)} %bitcast.6, f32[32,32]{1,0:T(8,128)} %v_stream.1, ...), custom_call_target="tpu_custom_call" | custom-call | tf_op jit(solution)/shard_map/pallas_call | solution.py:322
  20.3 1.6 %copy.16 = f32[16,16,128]{2,1,0:T(8,128)} copy(f32[16,16,128]{2,1,0:T(8,128)} %shard_map.127) | data formatting | bytes 262144
Async XLA Ops:
  0.0 0.7 %copy-start = (f32[1,18,18]{2,0,1:T(1,128)S(1)}, f32[1,18,18]{2,0,1:T(1,128)}, u32[]{:S(2)}) copy-start(f32[1,18,18]{2,0,1:T(1,128)} %param.15) | copy-start | bytes 3892
where the time goes:
time: 22.1 us; the launch traced here: 21.9 us
  Pallas kernels  19 us (86%)
  local copies, waits for them, and re-layouts  2.87 us (13%)
    pallas_call x1, Pallas kernels, per_device(): pl.pallas_call(functools.partial(kernel, sizes), out_shape=jax.ShapeDtype...  19 us
    unnamed x4, local copies, waits for them, and re-layouts  2.87 us

commit v1 on v0

--- a/solution.py
+++ b/solution.py
@@ -56,12 +56,17 @@
 
 def kernel(
     sizes,
-    res, stream, normal, span, eig_x, eig_y, eig_z,
-    v_stream, v_normal, v_span, lev_x, lev_y, lev_z,
-    out,
-    rim, kh, kl, cx, back, got, parts, mine,
-    ssem, rsem,
+    *refs,
 ):
+    inputs, out = refs[:13], refs[13]
+    rim, kh, kl, cx, back, got, parts, mine, ssem, rsem, isem = refs[14:25]
+    held = refs[25:]
+    (
+        res, stream, normal, span, eig_x, eig_y, eig_z,
+        v_stream, v_normal, v_span, lev_x, lev_y, lev_z,
+    ) = held
+    for i in range(13):
+        pltpu.make_async_copy(inputs[i], held[i], isem.at[i]).start()
     nx, ny, nz = sizes
     block = stream.shape[0]
     n = block - 2
@@ -106,6 +111,8 @@
         guarded(dy, functools.partial(signal, {"ez": wrap(iz + dz, nz), "ey": iy + dy}))
     inner = jnp.where(iy > 0, 2, 0) + jnp.where(iy < ny - 1, 2, 0)
 
+    for i in range(13):
+        pltpu.make_async_copy(inputs[i], held[i], isem.at[i]).wait()
     data = res[...].reshape(main, length)
     row, col = iota((rows, block), 0), iota((rows, block), 1)
     low = row & (n - 1)
@@ -125,7 +132,7 @@
     to_r = onehot(bq == brow)
     to_q = onehot((bcol - block * bq == brow) & (bcol < block * block))
     span_l = dot3(split(span[...]), split(to_r))
-    normal_l = dot3(split(normal[0]), split(to_q))
+    normal_l = dot3(split(normal[...].reshape(block, block)), split(to_q))
     kmat = pick(sel_k, span_l) * pick(sel_j, normal_l)
     k_hi, k_lo = split(kmat)
     kh[...] = k_hi
@@ -319,10 +326,16 @@
     mn = ny * nz
     copies = 18 + nx + ny + nz - 3
     vmem = pl.BlockSpec(memory_space=pltpu.VMEM)
+    args = (
+        residual, local_stream, local_normal.transpose(1, 0, 2), local_span,
+        eigen_stream.reshape(1, -1), eigen_normal, eigen_span.reshape(1, -1), vertex_stream,
+        vertex_normal, vertex_span, level_stream.reshape(1, -1), level_normal.reshape(1, -1),
+        level_span.reshape(1, -1),
+    )
     return pl.pallas_call(
         functools.partial(kernel, sizes),
-        out_shape=jax.ShapeDtypeStruct(residual.shape, F32),
-        in_specs=[vmem] * 13,
+        out_shape=pltpu.VMEM(residual.shape, F32),
+        in_specs=[pl.BlockSpec(memory_space=pltpu.HBM)] * 13,
         out_specs=vmem,
         scratch_shapes=[
             pltpu.VMEM((rows - n * n, length), F32),
@@ -335,13 +348,12 @@
             pltpu.VMEM((3, mn, 128), F32),
             pltpu.SemaphoreType.DMA((copies,)),
             pltpu.SemaphoreType.DMA((copies,)),
-        ],
-        compiler_params=pltpu.CompilerParams(collective_id=0, has_side_effects=True),
-    )(
-        residual, local_stream, local_normal, local_span, eigen_stream.reshape(1, -1), eigen_normal,
-        eigen_span.reshape(1, -1), vertex_stream, vertex_normal, vertex_span,
-        level_stream.reshape(1, -1), level_normal.reshape(1, -1), level_span.reshape(1, -1),
-    )
+            pltpu.SemaphoreType.DMA((13,)),
+        ] + [pltpu.VMEM(a.shape, F32) for a in args],
+        compiler_params=pltpu.CompilerParams(
+            collective_id=0, has_side_effects=True
+        ),
+    )(*args)
 
 
 def solution(mesh):

time: 22.1 us -> 18.4 us (0.83)
  local copies, waits for them, and re-layouts: 2.87 us -> 0.66 us
  Pallas kernels: 19 us -> 17.6 us
    unnamed x4 -> x1, local copies, waits for them, and re-layouts: 2.87 us -> 0.66 us
    pallas_call x1, Pallas kernels: 19 us -> 17.6 us  [per_device(): pl.pallas_call(functools.partial(kernel, sizes), out_shape=pltpu.VMEM(res...]
where the time goes in v1:
time: 18.4 us; the launch traced here: 18.2 us
  Pallas kernels  17.6 us (96%)
  local copies, waits for them, and re-layouts  0.66 us (4%)
    pallas_call x1, Pallas kernels, per_device(): pl.pallas_call(functools.partial(kernel, sizes), out_shape=pltpu.VMEM(res...  17.6 us
    unnamed x1, local copies, waits for them, and re-layouts  0.66 us

profile of v1, /device:TPU:0, one launch (start us, length us, event | category | flops | bytes accessed | tf_op | source)
XLA Modules:
  0.0 18.2 jit_solution(8079214082940850633)
XLA Ops:
  0.0 17.6 %shard_map.127 = f32[16,16,128]{2,1,0:T(8,128)S(1)} custom-call(f32[16,16,128]{2,1,0:T(8,128)} %refs_0_.1, f32[18,18]{1,0:T(8,128)} %refs_1_.1, f32[18,1,18]{2,1,0:T(1,128)} %bitcast.6, f32[18,18]{1,0:T(8,128)} %refs_3_.1, f32[1,18]{1,0:T(1,128)} %bitcast.7, f32[1,18]{1,0:T(1,128)} %refs_5_.1, f32[1,18]{1,0:T(1,128)} %bitcast.8, f32[32,32]{1,0:T(8,128)} %refs_7_.1, ...), custom_call_target="tpu_custom_call" | custom-call | tf_op jit(solution)/shard_map/pallas_call | solution.py:335
  17.6 0.7 %copy.15 = f32[16,16,128]{2,1,0:T(8,128)} copy(f32[16,16,128]{2,1,0:T(8,128)S(1)} %shard_map.127) | data formatting | bytes 262144

commit v2 on v1

--- a/solution.py
+++ b/solution.py
@@ -11,7 +11,6 @@
 F32 = jnp.float32
 BF16 = jnp.bfloat16
 I32 = jnp.int32
-HALO = 24
 DIRS = ((1, 0), (-1, 0), (0, 1), (0, -1), (1, 1), (1, -1), (-1, 1), (-1, -1))
 
 
@@ -59,8 +58,8 @@
     *refs,
 ):
     inputs, out = refs[:13], refs[13]
-    rim, kh, kl, cx, back, got, parts, mine, ssem, rsem, isem = refs[14:25]
-    held = refs[25:]
+    rim, kh, kl, cx, back, got, parts, mine, hx, vs, vr, us, ssem, rsem, isem = refs[14:29]
+    held = refs[29:]
     (
         res, stream, normal, span, eig_x, eig_y, eig_z,
         v_stream, v_normal, v_span, lev_x, lev_y, lev_z,
@@ -84,6 +83,7 @@
 
     rim[...] = jnp.zeros_like(rim)
     got[...] = jnp.zeros_like(got)
+    hx[...] = jnp.zeros_like(hx)
 
     def wrap(i, size):
         return lax.rem(i + size, size)
@@ -147,8 +147,8 @@
     wx = hat(xrow & (n - 1), wn)
     base = ix * ne + (xrow >> sh)
     after = jnp.where(base + 1 >= nv, base + 1 - nv, base + 1)
-    hx = jnp.where(xcol == base, 1.0 - wx, 0.0) + jnp.where(xcol == after, wx, 0.0)
-    wxm = split(dot3(split(hx), split(v_stream[...])))
+    hatx = jnp.where(xcol == base, 1.0 - wx, 0.0) + jnp.where(xcol == after, wx, 0.0)
+    wxm = split(dot3(split(hatx), split(v_stream[...])))
     d_split = split(data)
     loads = dot3(split(dot3(hyz, d_split)), wxm)
     mrow, mcol = iota((mn, nz), 0), iota((mn, nz), 1)
@@ -225,7 +225,7 @@
         st, index, size = stages[axis]
         return [
             shipped(
-                mine.at[st], parts.at[offset[axis] + d - 1], 18 + offset[axis] + d - 1,
+                mine.at[st], parts.at[offset[axis] + d - 1], 20 + offset[axis] + d - 1,
                 {axis: lax.rem(index + d, size)},
             )
             for d in range(1, size)
@@ -249,14 +249,18 @@
     k_main = kh[0:main], kl[0:main]
     k_rim = kh[main:], kl[main:]
     c_main = dot3(split(data.T), k_main)
-    nep = cx.shape[0]
-    pairs = (ne + 2) * block
+    nep = length + 16
+    pairs = ne * block
     npad = -(-pairs // 16) * 16
+
+    def place(c):
+        far = jnp.where(c == length + 8, length, -n * length)
+        return jnp.where(c < length, c, jnp.where(c == length, -1, far))
+
     wrow, wcol = iota((npad, nep), 0), iota((npad, nep), 1)
-    xs = jnp.where(wcol < length, wcol, jnp.where(wcol < length + HALO, wcol - length - HALO, wcol - HALO))
-    xi = xs + 1 + n - n * quotient(wrow, block)
+    xi = place(wcol) + 1 - n * quotient(wrow, block)
     trow, tcol = iota((block, nep), 0), iota((block, nep), 1)
-    tx = jnp.where(tcol < length, tcol, jnp.where(tcol < length + HALO, tcol - length - HALO, tcol - HALO))
+    tx = place(tcol)
     tm = (tx + 1) & (n - 1)
     s_t = split(stream[...].T)
     first = dot3(s_t, split(onehot(trow == tm)))
@@ -267,33 +271,51 @@
     wmat = wmat + jnp.where((xi >= n) & (xi < block), pick(is_p, second), 0.0)
     w_main = split(wmat[:, :length])
     w_halo = split(wmat[:, length:])
+    w_out = wmat[:, length:].T
     w_back = split(wmat[:, :length].T)
     eig_yz = dot3(split(jnp.broadcast_to(eig_z[...], (8, block))), split(to_r))
     eig_yz = eig_yz + dot3(split(jnp.broadcast_to(eig_y[...], (8, block))), split(to_q))
     ecol = jnp.sum(is_p * eig_x[...], axis=1, keepdims=True)
     ecol = jnp.where(iota((npad, 1), 0) < pairs, ecol, 1.0)
     inverse = 1.0 / (ecol + eig_yz[0:1])
+    own = dot3(split(w_out * w_out), split(inverse))
+    w_out = split(w_out)
 
     wait_all(halo)
-    cx[0:length] = c_main + dot3(split(rim[...].T), k_rim)
+    cx[...] = c_main + dot3(split(rim[...].T), k_rim)
+
+    right = {"ex": wrap(ix + 1, nx)}
+    left = {"ex": wrap(ix - 1, nx)}
 
     def x_copies():
-        right = {"ex": wrap(ix + 1, nx)}
-        left = {"ex": wrap(ix - 1, nx)}
         return (
-            shipped(cx.at[pl.ds(length - HALO, HALO)], cx.at[pl.ds(length, HALO)], 16, right),
-            shipped(cx.at[pl.ds(0, HALO)], cx.at[pl.ds(length + HALO, HALO)], 17, left),
+            shipped(cx.at[pl.ds(length - 1, 1)], hx.at[pl.ds(0, 1)], 16, right),
+            shipped(cx.at[pl.ds(0, 1)], hx.at[pl.ds(8, 1)], 17, left),
+        )
+
+    def v_copies():
+        return (
+            shipped(vs.at[pl.ds(8, 1)], vr.at[pl.ds(0, 1)], 18, right),
+            shipped(vs.at[pl.ds(0, 1)], vr.at[pl.ds(8, 1)], 19, left),
         )
 
     for c in x_copies():
+        c.start()
+    modal = dot3(w_main, split(cx[...]))
+    vs[...] = dot3(w_out, split(modal * inverse))
+    for c in v_copies():
         c.start()
     mine[1, :, :nm] = stage_end("ez")
     stage_start("ex")
-    modal = dot3(w_main, split(cx[0:length]))
     for c in x_copies():
         c.wait()
-    modal = modal + dot3(w_halo, split(cx[length:]))
-    u = split(dot3(w_back, split(modal * inverse)))
+    modal = modal + dot3(w_halo, split(hx[...]))
+    us[...] = dot3(w_back, split(modal * inverse))
+    for c in v_copies():
+        c.wait()
+    us[0:1] += vr[0:1] + own[8:9] * cx[0:1]
+    us[length - 1 : length] += vr[8:9] + own[0:1] * cx[length - 1 : length]
+    u = split(us[...])
     back[...] = dot3(k_rim, u, (1, 1))
     start_all(ret)
     mine[2, :, :nm] = stage_end("ex")
@@ -324,7 +346,7 @@
     rows = n * n + 4 * n + 16
     lanes = -(-block * block // 128) * 128
     mn = ny * nz
-    copies = 18 + nx + ny + nz - 3
+    copies = 20 + nx + ny + nz - 3
     vmem = pl.BlockSpec(memory_space=pltpu.VMEM)
     args = (
         residual, local_stream, local_normal.transpose(1, 0, 2), local_span,
@@ -341,11 +363,15 @@
             pltpu.VMEM((rows - n * n, length), F32),
             pltpu.VMEM((rows, lanes), BF16),
             pltpu.VMEM((rows, lanes), BF16),
-            pltpu.VMEM((length + 2 * HALO, lanes), F32),
+            pltpu.VMEM((length, lanes), F32),
             pltpu.VMEM((rows - n * n, length), F32),
             pltpu.VMEM((rows - n * n, length), F32),
             pltpu.VMEM((nx + ny + nz - 3, mn, 128), F32),
             pltpu.VMEM((3, mn, 128), F32),
+            pltpu.VMEM((16, lanes), F32),
+            pltpu.VMEM((16, lanes), F32),
+            pltpu.VMEM((16, lanes), F32),
+            pltpu.VMEM((length, lanes), F32),
             pltpu.SemaphoreType.DMA((copies,)),
             pltpu.SemaphoreType.DMA((copies,)),
             pltpu.SemaphoreType.DMA((13,)),

time: 18.4 us -> 17.7 us (0.962)
  Pallas kernels: 17.6 us -> 16.9 us
    pallas_call x1, Pallas kernels: 17.6 us -> 16.9 us  [per_device(): pl.pallas_call(functools.partial(kernel, sizes), out_shape=pltpu.VMEM(res...]
where the time goes in v2:
time: 17.7 us; the launch traced here: 17.5 us
  Pallas kernels  16.9 us (95%)
  local copies, waits for them, and re-layouts  0.66 us (4%)
    pallas_call x1, Pallas kernels, per_device(): pl.pallas_call(functools.partial(kernel, sizes), out_shape=pltpu.VMEM(res...  16.9 us
    unnamed x1, local copies, waits for them, and re-layouts  0.66 us

profile of v2, /device:TPU:0, one launch (start us, length us, event | category | flops | bytes accessed | tf_op | source)
XLA Modules:
  0.0 17.5 jit_solution(238961060512130069)
XLA Ops:
  0.0 16.9 %shard_map.127 = f32[16,16,128]{2,1,0:T(8,128)S(1)} custom-call(f32[16,16,128]{2,1,0:T(8,128)} %refs_0_.1, f32[18,18]{1,0:T(8,128)} %refs_1_.1, f32[18,1,18]{2,1,0:T(1,128)} %bitcast.6, f32[18,18]{1,0:T(8,128)} %refs_3_.1, f32[1,18]{1,0:T(1,128)} %bitcast.7, f32[1,18]{1,0:T(1,128)} %refs_5_.1, f32[1,18]{1,0:T(1,128)} %bitcast.8, f32[32,32]{1,0:T(8,128)} %refs_7_.1, ...), custom_call_target="tpu_custom_call" | custom-call | tf_op jit(solution)/shard_map/pallas_call | solution.py:357
  16.9 0.7 %copy.15 = f32[16,16,128]{2,1,0:T(8,128)} copy(f32[16,16,128]{2,1,0:T(8,128)S(1)} %shard_map.127) | data formatting | bytes 262144

commit v3 on v2

--- a/solution.py
+++ b/solution.py
@@ -111,7 +111,85 @@
         guarded(dy, functools.partial(signal, {"ez": wrap(iz + dz, nz), "ey": iy + dy}))
     inner = jnp.where(iy > 0, 2, 0) + jnp.where(iy < ny - 1, 2, 0)
 
-    for i in range(13):
+    pltpu.make_async_copy(inputs[0], held[0], isem.at[0]).wait()
+    pl.semaphore_wait(barrier, (nx - 1) + (ny - 1) + (nz - 1) + inner)
+
+    def shipped(src, dst, slot, where):
+        return pltpu.make_async_remote_copy(
+            src_ref=src, dst_ref=dst, send_sem=ssem.at[slot], recv_sem=rsem.at[slot],
+            device_id=where, device_id_type=pl.DeviceIdType.MESH,
+        )
+
+    def target(dz, dy):
+        where = {}
+        if dz:
+            where["ez"] = wrap(iz + dz, nz)
+        if dy:
+            where["ey"] = iy + dy
+        return where
+
+    def halo(slot):
+        dz, dy = DIRS[slot]
+        if dy == 0:
+            src = res.at[n - 1 if dz > 0 else 0]
+            dst = rim.at[pl.ds(0 if dz > 0 else n, n)]
+        elif dz == 0:
+            src = res.at[:, n - 1 if dy > 0 else 0]
+            dst = rim.at[pl.ds(2 * n if dy > 0 else 3 * n, n)]
+        else:
+            src = res.at[n - 1 if dz > 0 else 0, pl.ds(n - 1 if dy > 0 else 0, 1)]
+            dst = rim.at[pl.ds(4 * n + (0 if dz > 0 else 2) + (0 if dy > 0 else 1), 1)]
+        return shipped(src, dst, slot, target(dz, dy))
+
+    def ret(slot):
+        dz, dy = DIRS[slot]
+        if dy == 0:
+            at, number = (n if dz > 0 else 0), n
+        elif dz == 0:
+            at, number = (3 * n if dy > 0 else 2 * n), n
+        else:
+            at, number = 4 * n + (2 if dz > 0 else 0) + (1 if dy > 0 else 0), 1
+        return shipped(
+            back.at[pl.ds(at, number)], got.at[pl.ds(at, number)], 8 + slot, target(dz, dy)
+        )
+
+    def start_all(make):
+        for s, (dz, dy) in enumerate(DIRS):
+            guarded(dy, lambda s=s: make(s).start())
+
+    def wait_all(make):
+        for s, (dz, dy) in enumerate(DIRS):
+            guarded(dy, lambda s=s: make(s).wait_send())
+            guarded(-dy, lambda s=s: make(s).wait_recv())
+
+    stages = {"ez": (0, iz, nz), "ex": (1, ix, nx), "ey": (2, iy, ny)}
+    offset = {"ez": 0, "ex": nz - 1, "ey": nz + nx - 2}
+
+    def stage_copies(axis):
+        st, index, size = stages[axis]
+        return [
+            shipped(
+                mine.at[st], parts.at[offset[axis] + d - 1], 20 + offset[axis] + d - 1,
+                {axis: lax.rem(index + d, size)},
+            )
+            for d in range(1, size)
+        ]
+
+    def stage_start(axis):
+        for c in stage_copies(axis):
+            c.start()
+
+    def stage_end(axis):
+        st, index, size = stages[axis]
+        total = mine[st, :, :nm]
+        for d, c in enumerate(stage_copies(axis)):
+            c.wait_recv()
+            c.wait_send()
+            total = total + parts[offset[axis] + d, :, :nm]
+        return total
+
+    start_all(halo)
+    for i in range(1, 13):
         pltpu.make_async_copy(inputs[i], held[i], isem.at[i]).wait()
     data = res[...].reshape(main, length)
     row, col = iota((rows, block), 0), iota((rows, block), 1)
@@ -168,83 +246,6 @@
     level = jnp.sum(is_m * lev_z[...], axis=1, keepdims=True)
     level = level + jnp.sum(is_n * lev_y[...], axis=1, keepdims=True) + lev_x[...]
 
-    pl.semaphore_wait(barrier, (nx - 1) + (ny - 1) + (nz - 1) + inner)
-
-    def shipped(src, dst, slot, where):
-        return pltpu.make_async_remote_copy(
-            src_ref=src, dst_ref=dst, send_sem=ssem.at[slot], recv_sem=rsem.at[slot],
-            device_id=where, device_id_type=pl.DeviceIdType.MESH,
-        )
-
-    def target(dz, dy):
-        where = {}
-        if dz:
-            where["ez"] = wrap(iz + dz, nz)
-        if dy:
-            where["ey"] = iy + dy
-        return where
-
-    def halo(slot):
-        dz, dy = DIRS[slot]
-        if dy == 0:
-            src = res.at[n - 1 if dz > 0 else 0]
-            dst = rim.at[pl.ds(0 if dz > 0 else n, n)]
-        elif dz == 0:
-            src = res.at[:, n - 1 if dy > 0 else 0]
-            dst = rim.at[pl.ds(2 * n if dy > 0 else 3 * n, n)]
-        else:
-            src = res.at[n - 1 if dz > 0 else 0, pl.ds(n - 1 if dy > 0 else 0, 1)]
-            dst = rim.at[pl.ds(4 * n + (0 if dz > 0 else 2) + (0 if dy > 0 else 1), 1)]
-        return shipped(src, dst, slot, target(dz, dy))
-
-    def ret(slot):
-        dz, dy = DIRS[slot]
-        if dy == 0:
-            at, number = (n if dz > 0 else 0), n
-        elif dz == 0:
-            at, number = (3 * n if dy > 0 else 2 * n), n
-        else:
-            at, number = 4 * n + (2 if dz > 0 else 0) + (1 if dy > 0 else 0), 1
-        return shipped(
-            back.at[pl.ds(at, number)], got.at[pl.ds(at, number)], 8 + slot, target(dz, dy)
-        )
-
-    def start_all(make):
-        for s, (dz, dy) in enumerate(DIRS):
-            guarded(dy, lambda s=s: make(s).start())
-
-    def wait_all(make):
-        for s, (dz, dy) in enumerate(DIRS):
-            guarded(dy, lambda s=s: make(s).wait_send())
-            guarded(-dy, lambda s=s: make(s).wait_recv())
-
-    stages = {"ez": (0, iz, nz), "ex": (1, ix, nx), "ey": (2, iy, ny)}
-    offset = {"ez": 0, "ex": nz - 1, "ey": nz + nx - 2}
-
-    def stage_copies(axis):
-        st, index, size = stages[axis]
-        return [
-            shipped(
-                mine.at[st], parts.at[offset[axis] + d - 1], 20 + offset[axis] + d - 1,
-                {axis: lax.rem(index + d, size)},
-            )
-            for d in range(1, size)
-        ]
-
-    def stage_start(axis):
-        for c in stage_copies(axis):
-            c.start()
-
-    def stage_end(axis):
-        st, index, size = stages[axis]
-        total = mine[st, :, :nm]
-        for d, c in enumerate(stage_copies(axis)):
-            c.wait_recv()
-            c.wait_send()
-            total = total + parts[offset[axis] + d, :, :nm]
-        return total
-
-    start_all(halo)
     stage_start("ez")
     k_main = kh[0:main], kl[0:main]
     k_rim = kh[main:], kl[main:]

time: 17.7 us -> 17.5 us (0.989)
  Pallas kernels: 16.9 us -> 16.7 us
where the time goes in v3:
time: 17.5 us; the launch traced here: 17.4 us
  Pallas kernels  16.7 us (95%)
  local copies, waits for them, and re-layouts  0.66 us (4%)
    pallas_call x1, Pallas kernels, per_device(): pl.pallas_call(functools.partial(kernel, sizes), out_shape=pltpu.VMEM(res...  16.7 us
    unnamed x1, local copies, waits for them, and re-layouts  0.66 us

profile of v3, /device:TPU:0, one launch (start us, length us, event | category | flops | bytes accessed | tf_op | source)
XLA Modules:
  0.0 17.4 jit_solution(5028711860833793194)
XLA Ops:
  0.0 16.7 %shard_map.127 = f32[16,16,128]{2,1,0:T(8,128)S(1)} custom-call(f32[16,16,128]{2,1,0:T(8,128)} %refs_0_.1, f32[18,18]{1,0:T(8,128)} %refs_1_.1, f32[18,1,18]{2,1,0:T(1,128)} %bitcast.6, f32[18,18]{1,0:T(8,128)} %refs_3_.1, f32[1,18]{1,0:T(1,128)} %bitcast.7, f32[1,18]{1,0:T(1,128)} %refs_5_.1, f32[1,18]{1,0:T(1,128)} %bitcast.8, f32[32,32]{1,0:T(8,128)} %refs_7_.1, ...), custom_call_target="tpu_custom_call" | custom-call | tf_op jit(solution)/shard_map/pallas_call | solution.py:358
  16.7 0.7 %copy.15 = f32[16,16,128]{2,1,0:T(8,128)} copy(f32[16,16,128]{2,1,0:T(8,128)S(1)} %shard_map.127) | data formatting | bytes 262144

commit v4 on v3

--- a/solution.py
+++ b/solution.py
@@ -162,7 +162,7 @@
             guarded(dy, lambda s=s: make(s).wait_send())
             guarded(-dy, lambda s=s: make(s).wait_recv())
 
-    stages = {"ez": (0, iz, nz), "ex": (1, ix, nx), "ey": (2, iy, ny)}
+    stages = {"ex": (0, ix, nx), "ez": (1, iz, nz), "ey": (2, iy, ny)}
     offset = {"ez": 0, "ex": nz - 1, "ey": nz + nx - 2}
 
     def stage_copies(axis):
@@ -246,7 +246,7 @@
     level = jnp.sum(is_m * lev_z[...], axis=1, keepdims=True)
     level = level + jnp.sum(is_n * lev_y[...], axis=1, keepdims=True) + lev_x[...]
 
-    stage_start("ez")
+    stage_start("ex")
     k_main = kh[0:main], kl[0:main]
     k_rim = kh[main:], kl[main:]
     c_main = dot3(split(data.T), k_main)
@@ -306,8 +306,10 @@
     vs[...] = dot3(w_out, split(modal * inverse))
     for c in v_copies():
         c.start()
-    mine[1, :, :nm] = stage_end("ez")
-    stage_start("ex")
+    mine[1, :, :nm] = stage_end("ex")
+    stage_start("ez")
+    mine[2, :, :nm] = stage_end("ez")
+    stage_start("ey")
     for c in x_copies():
         c.wait()
     modal = modal + dot3(w_halo, split(hx[...]))
@@ -319,8 +321,6 @@
     u = split(us[...])
     back[...] = dot3(k_rim, u, (1, 1))
     start_all(ret)
-    mine[2, :, :nm] = stage_end("ex")
-    stage_start("ey")
     result = dot3(k_main, u, (1, 1))
     scaled = split(stage_end("ey") / level)
     coarse = dot3(split(amat.T), scaled)

time: 17.5 us -> 17.3 us (0.989)
  Pallas kernels: 16.7 us -> 16.5 us
    pallas_call x1, Pallas kernels: 16.7 us -> 16.5 us  [per_device(): pl.pallas_call(functools.partial(kernel, sizes), out_shape=pltpu.VMEM(res...]
where the time goes in v4:
time: 17.3 us; the launch traced here: 17.2 us
  Pallas kernels  16.5 us (95%)
  local copies, waits for them, and re-layouts  0.66 us (4%)
    pallas_call x1, Pallas kernels, per_device(): pl.pallas_call(functools.partial(kernel, sizes), out_shape=pltpu.VMEM(res...  16.5 us
    unnamed x1, local copies, waits for them, and re-layouts  0.66 us

profile of v4, /device:TPU:0, one launch (start us, length us, event | category | flops | bytes accessed | tf_op | source)
XLA Modules:
  0.0 17.2 jit_solution(4049092227299143987)
XLA Ops:
  0.0 16.5 %shard_map.127 = f32[16,16,128]{2,1,0:T(8,128)S(1)} custom-call(f32[16,16,128]{2,1,0:T(8,128)} %refs_0_.1, f32[18,18]{1,0:T(8,128)} %refs_1_.1, f32[18,1,18]{2,1,0:T(1,128)} %bitcast.6, f32[18,18]{1,0:T(8,128)} %refs_3_.1, f32[1,18]{1,0:T(1,128)} %bitcast.7, f32[1,18]{1,0:T(1,128)} %refs_5_.1, f32[1,18]{1,0:T(1,128)} %bitcast.8, f32[32,32]{1,0:T(8,128)} %refs_7_.1, ...), custom_call_target="tpu_custom_call" | custom-call | tf_op jit(solution)/shard_map/pallas_call | solution.py:358
  16.5 0.7 %copy.15 = f32[16,16,128]{2,1,0:T(8,128)} copy(f32[16,16,128]{2,1,0:T(8,128)S(1)} %shard_map.127) | data formatting | bytes 262144
